TPU v7x, 512 devices: a whole 4x8x8 slice. The times are simulated.
512 devices in a mesh: row: 16 (over z, core), col: 32 (over y, x).
Axes of the slice: x: 4, y: 8, z: 8, core: 2. Of those that a mesh axis runs over, the one named last changes fastest.
Arguments:
- initial_voltage: float32 [16, 64, 128, 128], P('row', 'col'), may hold values from -6 to 6
- inject: float32 [16, 64, 128, 128], P('row', 'col'), may hold values from -6 to 6
- conduct: float32 [16, 64, 128, 128], P('row', 'col'), as said below
- capacitance: float32 [16, 64, 128], P('row', 'col'), may hold values from 1 to 4
- track_gain: float32 [16, 64, 2, 32], P('row', 'col'), may hold values from 0.3 to 3
- driver_tile: int32 [16, 32, 64], P('row', 'col'), may hold values from 0 to 1
- sink_net: int32 [16, 32, 32, 8], P('row', 'col'), may hold values from 0 to 63
- sink_count: int32 [16, 32, 32], P('row', 'col'), may hold values from 0 to 8, as said below
- sink_tile: int32 [16, 32, 32, 8], P('row', 'col'), may hold values from 0 to 1
- sink_node: int32 [16, 32, 32, 8], P('row', 'col'), may hold values from 0 to 127
- sink_gain: float32 [16, 32, 32, 8], P('row', 'col'), may hold values from 0.5 to 2
Outputs:
- voltage: float32 [16, 64, 128, 128], P('row', 'col')
Inputs may be any that keep to these rules, and one draw needn't show every extreme that they name: Slots k >= sink_count[d, s] are ignored; some receiving device takes all 8 slots from some source device in every draw. `conduct`: each tile's block is symmetric with non-positive entries off the diagonal and rows summing to zero.
All inputs are finite; a program needn't handle non-finite values.
Results may differ from a plain program's by a relative error of at most 0.0001.
Values sent between devices are 32-bit elements; how exact they have to be, the bound alone decides.
A program may use at most 64 MiB of HBM per device.

v0:
```python
import jax
import jax.numpy as jnp
from jax import lax
from jax.sharding import PartitionSpec as P

ITERS = 3
PRECISE = lax.Precision.HIGHEST


def padded_2(block, sides, width):
    for axis, dim in sides:
        count = lax.axis_size(axis)
        forward = [(i, i + 1) for i in range(count - 1)]
        backward = [(target, source) for source, target in forward]
        low = lax.ppermute(
            lax.slice_in_dim(block, block.shape[dim] - width, None, axis=dim), axis, forward
        )
        high = lax.ppermute(lax.slice_in_dim(block, 0, width, axis=dim), axis, backward)
        block = jnp.concatenate([low, block, high], axis=dim)
    return block


def shifted(block, axis, distance):
    devices = range(lax.axis_size(axis))
    route = [(i - distance, i) for i in devices if i - distance in devices]
    return lax.ppermute(block, axis, route)


def tile_inverse(conduct, capacitance):
    node_count = conduct.shape[-1]
    identity = jnp.eye(node_count, dtype=jnp.float32)
    whole_block = conduct + capacitance[..., None] * identity
    flat_blocks = whole_block.reshape((-1, node_count, node_count))
    factors = jnp.linalg.cholesky(flat_blocks)
    inverse = jax.vmap(lambda factor: jax.scipy.linalg.cho_solve((factor, True), identity))(factors)
    return inverse.reshape(whole_block.shape)


def apply_grid(voltage, conduct, capacitance, track_pad):
    edge_count = track_pad.shape[-1]
    inner_part = (
        jnp.einsum("rcij,rcjp->rcip", conduct, voltage, precision=PRECISE)
        + capacitance[..., None] * voltage
    )
    rim_cells = voltage[:, :, :edge_count, :]
    padded = padded_2(rim_cells, (("row", 0), ("col", 1)), 1)
    east_gain = track_pad[1:-1, 1:-1, 0][..., None]
    west_gain = track_pad[1:-1, :-2, 0][..., None]
    south_gain = track_pad[1:-1, 1:-1, 1][..., None]
    north_gain = track_pad[:-2, 1:-1, 1][..., None]
    track_flow = east_gain * (rim_cells - padded[1:-1, 2:]) + west_gain * (
        rim_cells - padded[1:-1, :-2]
    )
    track_flow = (
        track_flow
        + south_gain * (rim_cells - padded[2:, 1:-1])
        + north_gain * (rim_cells - padded[:-2, 1:-1])
    )
    return jnp.concatenate(
        [inner_part[:, :, :edge_count] + track_flow, inner_part[:, :, edge_count:]], axis=2
    )


def precondition(inverse, residual):
    return jnp.einsum("rcij,rcjp->rcip", inverse, residual, precision=PRECISE)


def inner_sum(left_vec, right_vec):
    return jnp.sum(left_vec * right_vec, axis=(0, 1, 2))


def residual_product(residual, precond):
    return lax.psum(inner_sum(residual, precond), ("row", "col"))


def solve_separate(right_side, initial, conduct, capacitance, track_pad, inverse):
    solution = initial
    residual = right_side - apply_grid(initial, conduct, capacitance, track_pad)
    precond = precondition(inverse, residual)
    direction = precond
    rz_now = residual_product(residual, precond)
    for sweep_idx in range(ITERS):
        applied = apply_grid(direction, conduct, capacitance, track_pad)
        curvature = lax.psum(inner_sum(direction, applied), ("row", "col"))
        step_size = rz_now / curvature
        solution = solution + step_size * direction
        residual = residual - step_size * applied
        precond = precondition(inverse, residual)
        rz_fresh = residual_product(residual, precond)
        direction = precond + rz_fresh / rz_now * direction
        rz_now = rz_fresh
    return solution


def driver_voltage(voltage, driver_tile):
    node_count = voltage.shape[2]
    flat_field = voltage.reshape((-1, voltage.shape[3]))
    net_count = driver_tile.shape[-1]
    row_index = (
        driver_tile.reshape(-1) * node_count + jnp.arange(net_count, dtype=jnp.int32) % node_count
    )
    return jnp.take(flat_field, row_index, axis=0)


def sink_current(values, sink_tile, sink_node, sink_gain, sink_count, node_count, tile_count):
    source_count, slot_count, pattern_count = values.shape
    live_slot = jnp.arange(slot_count, dtype=jnp.int32)[None, :] < sink_count.reshape(
        (source_count, 1)
    )
    weight = jnp.where(live_slot, sink_gain.reshape((source_count, slot_count)), jnp.float32(0.0))
    row_index = (sink_tile * node_count + sink_node).reshape(-1)
    scaled = (values * weight[..., None]).reshape((-1, pattern_count))
    injected = jnp.zeros((tile_count * node_count, pattern_count), jnp.float32)
    return injected.at[row_index].add(scaled)


def lower_rims(track_gain):
    west_piece = shifted(track_gain[:, -1:, 0, :], "col", 1)
    north_piece = shifted(track_gain[-1:, :, 1, :], "row", 1)
    track_pad = jnp.pad(track_gain, ((1, 1), (1, 1), (0, 0), (0, 0)))
    track_pad = track_pad.at[1:-1, 0, 0].set(west_piece[:, 0])
    return track_pad.at[0, 1:-1, 1].set(north_piece[0])


def local(
    initial_voltage,
    inject,
    conduct,
    capacitance,
    track_gain,
    driver_tile,
    sink_net,
    sink_count,
    sink_tile,
    sink_node,
    sink_gain,
):
    inverse = tile_inverse(conduct, capacitance)
    track_pad = lower_rims(track_gain)
    col_count = lax.axis_size("col")
    net_count = driver_tile.shape[-1]
    pattern_count = initial_voltage.shape[3]
    node_count = initial_voltage.shape[2]
    tile_count = initial_voltage.shape[0] * initial_voltage.shape[1]
    wanted = sink_net.reshape((sink_net.shape[2], sink_net.shape[3]))
    voltage = initial_voltage
    drivers = driver_voltage(voltage, driver_tile)
    gathered = lax.all_gather(drivers, "col", axis=0, tiled=True)
    offsets = jnp.arange(col_count, dtype=jnp.int32)[:, None] * net_count
    values = jnp.take(gathered, (wanted + offsets).reshape(-1), axis=0).reshape(
        wanted.shape + (pattern_count,)
    )
    injected = sink_current(
        values, sink_tile, sink_node, sink_gain, sink_count, node_count, tile_count
    )
    right_side = capacitance[..., None] * voltage + inject + injected.reshape(voltage.shape)
    voltage = solve_separate(right_side, voltage, conduct, capacitance, track_pad, inverse)
    return voltage


def solution(mesh):
    placed = (
        P("row", "col", None, None),
        P("row", "col", None, None),
        P("row", "col", None, None),
        P("row", "col", None),
        P("row", "col", None, None),
        P("row", "col", None),
        P("row", "col", None, None),
        P("row", "col", None),
        P("row", "col", None, None),
        P("row", "col", None, None),
        P("row", "col", None, None),
    )
    return jax.shard_map(
        local, mesh=mesh, in_specs=placed, out_specs=P("row", "col", None, None), check_vma=False
    )
```

profile of v0, /device:TPU:1, one launch (start us, length us, event | category | flops | bytes accessed | tf_op | source)
XLA Modules:
  0.0 707.5 jit_solution(17942465035946714458)
XLA Ops:
  6.5 1.1 copy.150
  7.6 8.8 %collective-permute-start.2 = (f32[1,2,32,128]{2,3,1,0:T(8,128)S(1)}, f32[1,2,32,128]{2,3,1,0:T(8,128)S(1)}, u32[]{:S(2)}, u32[]{:S(2)}) collective-permute-start(f32[1,2,32,128]{2,3,1,0:T(8,128)S(1)} %bitcast.150), channel_id=1, source_target_pairs={{32,0},{64,32},{96,64},{128,96},{160,128},{192,160},{224,192},{256... | collective-permute-start | bytes 98312 | tf_op jit(solution)/shard_map/ppermute | solution.py:18
  16.4 1.9 collective-permute-start.1
  18.4 1.3 collective-permute-start
  19.7 1.9 collective-permute-start.5
  29.1 1.3 collective-permute-start.3
  30.4 4.0 collective-permute-start.4
  34.5 1.1 collective-permute-done.4
  35.9 66.4 %all-gather.2.cloned.1.call-done = f32[2048,128]{1,0:T(8,128)} async-done(((f32[64,128]{1,0:T(8,128)}), f32[2048,128]{1,0:T(8,128)}) %all-gather.2.cloned.1.call-update) | async-done | bytes 1048592 | tf_op jit(solution)/shard_map/all_gather | solution.py:148
  102.3 3.4 scatter_custom_fusion
  106.0 23.5 %custom-call.11 = f32[2,128,128]{2,1,0:T(8,128)S(1)} custom-call(f32[2,128,128]{2,1,0:T(8,128)S(1)} %fusion.13), custom_call_target="Cholesky" | custom-call | tf_op jit(solution)/shard_map/jit(cholesky)/cholesky | solution.py:34
  129.8 19.7 %custom-call.12 = f32[2,1,128,128]{2,3,1,0:T(8,128)S(1)} custom-call(f32[2,1,128,128]{3,2,1,0:T(8,128)S(1)} %select_bitcast_fusion), custom_call_target="InvertDiagBlocksLowerTriangular" | custom-call | tf_op jit(solution)/shard_map/vmap(jit(_cho_solve))/triangular_solve | solution.py:35
  151.0 6.9 collective-permute-start.7
  157.9 3.2 collective-permute-start.6
  161.9 1.2 collective-permute-done.6
  163.1 1.3 collective-permute-start.8
  164.4 4.0 collective-permute-start.9
  170.1 103.8 %all-reduce.1 = (f32[128]{0:T(128)S(1)}, f32[128]{0:T(128)S(1)}) all-reduce(f32[128]{0:T(128)S(1)} %multiply_reduce_fusion, f32[128]{0:T(128)S(1)} %fusion.8), channel_id=1, replica_groups=mesh['row'=16,'col'=32] {'row','col'}, use_global_device_ids=true, to_apply=%region_4.5 | all-reduce | flops 256 | bytes 2048 | tf_op jit(solution)/shard_map/psum | solution.py:73
  274.5 95.4 %psum.44 = f32[128]{0:T(128)S(1)} all-reduce(f32[128]{0:T(128)S(1)} %get-tuple-element.56), channel_id=1, replica_groups=mesh['row'=16,'col'=32] {'row','col'}, use_global_device_ids=true, to_apply=%region_8.9 | all-reduce | flops 128 | bytes 1024 | tf_op jit(solution)/shard_map/psum | solution.py:73
  370.0 2.6 collective-permute-start.11
  372.6 3.3 collective-permute-start.10
  376.7 1.2 collective-permute-done.10
  377.9 1.3 collective-permute-start.12
  379.2 4.0 collective-permute-start.13
  384.8 102.0 %psum.45 = f32[128]{0:T(128)S(1)} all-reduce(f32[128]{0:T(128)S(1)} %fusion.10), channel_id=1, replica_groups=mesh['row'=16,'col'=32] {'row','col'}, use_global_device_ids=true, to_apply=%region_10.11 | all-reduce | flops 128 | bytes 1024 | tf_op jit(solution)/shard_map/psum | solution.py:84
  487.4 95.3 %psum.46 = f32[128]{0:T(128)S(1)} all-reduce(f32[128]{0:T(128)S(1)} %get-tuple-element.58), channel_id=1, replica_groups=mesh['row'=16,'col'=32] {'row','col'}, use_global_device_ids=true, to_apply=%region_12.13 | all-reduce | flops 128 | bytes 1024 | tf_op jit(solution)/shard_map/psum | solution.py:73
  582.7 2.6 collective-permute-start.15
  585.3 3.5 collective-permute-start.14
  589.6 1.2 collective-permute-done.14
  590.8 1.3 collective-permute-start.16
  592.1 4.0 collective-permute-start.17
  597.8 102.0 %psum.47 = f32[128]{0:T(128)S(1)} all-reduce(f32[128]{0:T(128)S(1)} %fusion.12), channel_id=1, replica_groups=mesh['row'=16,'col'=32] {'row','col'}, use_global_device_ids=true, to_apply=%region_14.15 | all-reduce | flops 128 | bytes 1024 | tf_op jit(solution)/shard_map/psum | solution.py:84
  (144 shorter events, 19.2 us)
Async XLA Ops:
  6.5 15.1 %copy-start.1 = (f32[1,2,128,128]{3,2,1,0:T(8,128)S(1)}, f32[1,2,128,128]{3,2,1,0:T(8,128)}, u32[]{:S(2)}) copy-start(f32[1,2,128,128]{3,2,1,0:T(8,128)} %param.15) | copy-start | bytes 393220
  6.5 11.8 %copy-start.4 = (f32[1,2,2,32]{3,2,1,0:T(2,128)S(1)}, f32[1,2,2,32]{3,2,1,0:T(2,128)}, u32[]{:S(2)}) copy-start(f32[1,2,2,32]{3,2,1,0:T(2,128)} %param.19) | copy-start | bytes 1540
  6.5 95.8 %all-gather.2.cloned.1.call-start = ((), (), s32[]{:S(2)}) async-start(), calls=%async_computation | async-start | bytes 1081344 | tf_op jit(solution)/shard_map/all_gather | solution.py:148
  7.6 21.3 %collective-permute-start.2 = (f32[1,2,32,128]{2,3,1,0:T(8,128)S(1)}, f32[1,2,32,128]{2,3,1,0:T(8,128)S(1)}, u32[]{:S(2)}, u32[]{:S(2)}) collective-permute-start(f32[1,2,32,128]{2,3,1,0:T(8,128)S(1)} %bitcast.150), channel_id=1, source_target_pairs={{32,0},{64,32},{96,64},{128,96},{160,128},{192,160},{224,192},{256... | collective-permute-start | bytes 98312 | tf_op jit(solution)/shard_map/ppermute | solution.py:18
  16.4 12.6 %collective-permute-start.1 = (f32[1,2,32,128]{2,3,1,0:T(8,128)S(1)}, f32[1,2,32,128]{2,3,1,0:T(8,128)S(1)}, u32[]{:S(2)}, u32[]{:S(2)}) collective-permute-start(f32[1,2,32,128]{2,3,1,0:T(8,128)S(1)} %bitcast.151), channel_id=1, source_target_pairs={{0,32},{32,64},{64,96},{96,128},{128,160},{160,192},{192,224},{224... | collective-permute-start | bytes 98312 | tf_op jit(solution)/shard_map/ppermute | solution.py:15
  18.4 10.5 %collective-permute-start = (f32[1,1,32]{2,1,0:T(1,128)S(1)}, f32[1,1,32]{2,1,0:T(1,128)S(1)}, u32[]{:S(2)}, u32[]{:S(2)}) collective-permute-start(f32[1,1,32]{2,1,0:T(1,128)S(1)} %slice_bitcast_fusion.1), channel_id=1, source_target_pairs={{0,1},{1,2},{2,3},{3,4},{4,5},{5,6},{6,7},{7,8},{8,9},{9,10},{10,1... | collective-permute-start | bytes 392 | tf_op jit(solution)/shard_map/ppermute | solution.py:26
  19.7 1.9 copy-start.10
  19.7 16.1 %collective-permute-start.5 = (f32[1,2,32]{2,1,0:T(2,128)S(1)}, f32[1,2,32]{2,1,0:T(2,128)S(1)}, u32[]{:S(2)}, u32[]{:S(2)}) collective-permute-start(f32[1,2,32]{2,1,0:T(2,128)S(1)} %bitcast.184), channel_id=1, source_target_pairs={{0,32},{32,64},{64,96},{96,128},{128,160},{160,192},{192,224},{224... | collective-permute-start | bytes 776 | tf_op jit(solution)/shard_map/ppermute | solution.py:26
  23.2 0.7 copy-start.5
  23.8 2.7 copy-start
  24.1 0.7 copy-start.9
  24.8 0.7 copy-start.6
  24.8 0.7 copy-start.7
  25.6 0.7 copy-start.8
  26.5 0.7 copy-start.3
  27.9 0.9 copy-start.2
  29.1 5.3 collective-permute-start.3
  30.4 5.2 collective-permute-start.4
  151.0 10.8 %collective-permute-start.7 = (f32[1,2,32,128]{2,3,1,0:T(8,128)S(1)}, f32[1,2,32,128]{2,3,1,0:T(8,128)S(1)}, u32[]{:S(2)}, u32[]{:S(2)}) collective-permute-start(f32[1,2,32,128]{2,3,1,0:T(8,128)S(1)} %bitcast.142), channel_id=1, source_target_pairs={{32,0},{64,32},{96,64},{128,96},{160,128},{192,160},{224,192},{256... | collective-permute-start | bytes 98312 | tf_op jit(solution)/shard_map/ppermute | solution.py:18
  157.9 5.1 collective-permute-start.6
  163.1 5.4 collective-permute-start.8
  164.4 5.2 collective-permute-start.9
  370.0 6.6 collective-permute-start.11
  372.6 5.2 collective-permute-start.10
  377.9 5.4 collective-permute-start.12
  379.2 5.2 collective-permute-start.13
  582.7 6.8 collective-permute-start.15
  585.3 5.4 collective-permute-start.14
  590.8 5.4 collective-permute-start.16
  592.1 5.2 collective-permute-start.17
Sparse Core Ops, SparseCore 0:
  23.1 79.1 all-gather.1
where the time goes:
time: 709 us; the launch traced here: 707 us
  blocking collectives  498 us (70%)
  waiting for transfers between devices  75.2 us (11%)
  starting transfers between devices  57 us (8%)
  other arithmetic  49.2 us (7%)
  between operations  14.1 us (2%)
  local copies, waits for them, and re-layouts  9.8 us (1%)
    psum x3, blocking collectives, residual_product(): return lax.psum(inner_sum(residual, precond), ('row', 'col'))  295 us
    psum x2, blocking collectives, solve_separate(): curvature = lax.psum(inner_sum(direction, applied), ('row', 'col'))  204 us
    all_gather x1, waiting for transfers between devices, local(): gathered = lax.all_gather(drivers, 'col', axis=0, tiled=True)  66.4 us
    ppermute x8, starting transfers between devices, padded_2(): lax.ppermute(lax.slice_in_dim(block, block.shape[dim] - width, None, axis...  27.8 us
    ppermute x8, starting transfers between devices, padded_2(): lax.ppermute(lax.slice_in_dim(block, 0, width, axis=dim), axis, backward)  26 us
    another operation x4, other arithmetic, tile_inverse(): factors = jnp.linalg.cholesky(flat_blocks)  23.6 us
    another operation x3, other arithmetic, tile_inverse(): jax.scipy.linalg.cho_solve((factor, True), identity)  19.8 us
  transfers between devices with their start and end apart: 19, of which 11 were waited for; matrix products, arithmetic and copies ran while one was open for 1% of the time, Pallas kernels for 0%

commit v1 on v0

--- a/solution.py
+++ b/solution.py
@@ -70,7 +70,7 @@
 
 
 def residual_product(residual, precond):
-    return lax.psum(inner_sum(residual, precond), ("row", "col"))
+    return lax.psum(lax.psum(inner_sum(residual, precond), "row"), "col")
 
 
 def solve_separate(right_side, initial, conduct, capacitance, track_pad, inverse):

time: 709 us -> 797 us (1.12)
  blocking collectives: 498 us -> 562 us
  starting transfers between devices: 57 us -> 82.5 us
    psum x2 -> x3, blocking collectives: 204 us -> 312 us  [solve_separate(): curvature = lax.psum(inner_sum(direction, applied), ('row', 'col'))]
    psum x3 -> x6, blocking collectives: 295 us -> 249 us  [residual_product(): return lax.psum(lax.psum(inner_sum(residual, precond), 'row'), 'col')]
    ppermute x8, starting transfers between devices: 26 us -> 54.4 us  [padded_2(): lax.ppermute(lax.slice_in_dim(block, 0, width, axis=dim), axis, backward)]
  transfers between devices with their start and end apart: 19 -> 19, of which waited for: 11 -> 10; matrix products, arithmetic and copies ran while one was open for 1% -> 1% of each run, Pallas kernels for 0% -> 0%
where the time goes in v1:
time: 797 us; the launch traced here: 795 us
  blocking collectives  562 us (71%)
  starting transfers between devices  82.5 us (10%)
  waiting for transfers between devices  74.4 us (9%)
  other arithmetic  49.2 us (6%)
  between operations  14.1 us (2%)
  local copies, waits for them, and re-layouts  9.81 us (1%)
    psum x3, blocking collectives, solve_separate(): curvature = lax.psum(inner_sum(direction, applied), ('row', 'col'))  312 us
    psum x6, blocking collectives, residual_product(): return lax.psum(lax.psum(inner_sum(residual, precond), 'row'), 'col')  249 us
    all_gather x1, waiting for transfers between devices, local(): gathered = lax.all_gather(drivers, 'col', axis=0, tiled=True)  66.4 us
    ppermute x8, starting transfers between devices, padded_2(): lax.ppermute(lax.slice_in_dim(block, 0, width, axis=dim), axis, backward)  54.4 us
    ppermute x8, starting transfers between devices, padded_2(): lax.ppermute(lax.slice_in_dim(block, block.shape[dim] - width, None, axis...  24.9 us
    another operation x4, other arithmetic, tile_inverse(): factors = jnp.linalg.cholesky(flat_blocks)  23.6 us
    another operation x3, other arithmetic, tile_inverse(): jax.scipy.linalg.cho_solve((factor, True), identity)  19.8 us
  transfers between devices with their start and end apart: 19, of which 10 were waited for; matrix products, arithmetic and copies ran while one was open for 1% of the time, Pallas kernels for 0%

profile of v1, /device:TPU:1, one launch (start us, length us, event | category | flops | bytes accessed | tf_op | source)
XLA Modules:
  0.0 795.3 jit_solution(9317515298806243692)
XLA Ops:
  7.6 8.8 %collective-permute-start.2 = (f32[1,2,32,128]{2,3,1,0:T(8,128)S(1)}, f32[1,2,32,128]{2,3,1,0:T(8,128)S(1)}, u32[]{:S(2)}, u32[]{:S(2)}) collective-permute-start(f32[1,2,32,128]{2,3,1,0:T(8,128)S(1)} %bitcast.150), channel_id=1, source_target_pairs={{32,0},{64,32},{96,64},{128,96},{160,128},{192,160},{224,192},{256... | collective-permute-start | bytes 98312 | tf_op jit(solution)/shard_map/ppermute | solution.py:18
  16.4 1.9 collective-permute-start.1
  19.7 1.9 collective-permute-start.5
  29.1 1.3 collective-permute-start.3
  30.4 4.0 collective-permute-start.4
  35.9 66.4 %all-gather.2.cloned.1.call-done = f32[2048,128]{1,0:T(8,128)} async-done(((f32[64,128]{1,0:T(8,128)}), f32[2048,128]{1,0:T(8,128)}) %all-gather.2.cloned.1.call-update) | async-done | bytes 1048592 | tf_op jit(solution)/shard_map/all_gather | solution.py:148
  102.3 3.3 scatter_custom_fusion
  106.0 23.5 %custom-call.11 = f32[2,128,128]{2,1,0:T(8,128)S(1)} custom-call(f32[2,128,128]{2,1,0:T(8,128)S(1)} %fusion.13), custom_call_target="Cholesky" | custom-call | tf_op jit(solution)/shard_map/jit(cholesky)/cholesky | solution.py:34
  129.7 19.7 %custom-call.12 = f32[2,1,128,128]{2,3,1,0:T(8,128)S(1)} custom-call(f32[2,1,128,128]{3,2,1,0:T(8,128)S(1)} %select_bitcast_fusion), custom_call_target="InvertDiagBlocksLowerTriangular" | custom-call | tf_op jit(solution)/shard_map/vmap(jit(_cho_solve))/triangular_solve | solution.py:35
  151.0 7.0 collective-permute-start.7
  157.9 3.2 collective-permute-start.6
  163.1 1.3 collective-permute-start.8
  164.4 4.0 collective-permute-start.9
  168.5 25.7 %psum.63 = f32[128]{0:T(128)S(1)} all-reduce(f32[128]{0:T(128)S(1)} %multiply_reduce_fusion), channel_id=1, replica_groups=mesh['row'=16,'col'=32] {'row'}, use_global_device_ids=true, to_apply=%region_4.5 | all-reduce | flops 128 | bytes 1024 | tf_op jit(solution)/shard_map/psum | solution.py:73
  194.3 56.9 %psum.64 = f32[128]{0:T(128)S(1)} all-reduce(f32[128]{0:T(128)S(1)} %psum.63), channel_id=1, replica_groups=mesh['row'=16,'col'=32] {'col'}, use_global_device_ids=true, to_apply=%region_5.6 | all-reduce | flops 128 | bytes 1024 | tf_op jit(solution)/shard_map/psum | solution.py:73
  251.6 112.8 %psum.65 = f32[128]{0:T(128)S(1)} all-reduce(f32[128]{0:T(128)S(1)} %fusion.8), channel_id=1, replica_groups=mesh['row'=16,'col'=32] {'row','col'}, use_global_device_ids=true, to_apply=%region_7.8 | all-reduce | flops 128 | bytes 1024 | tf_op jit(solution)/shard_map/psum | solution.py:84
  365.0 23.6 %psum.66 = f32[128]{0:T(128)S(1)} all-reduce(f32[128]{0:T(128)S(1)} %get-tuple-element.54), channel_id=1, replica_groups=mesh['row'=16,'col'=32] {'row'}, use_global_device_ids=true, to_apply=%region_9.10 | all-reduce | flops 128 | bytes 1024 | tf_op jit(solution)/shard_map/psum | solution.py:73
  388.6 59.7 %psum.67 = f32[128]{0:T(128)S(1)} all-reduce(f32[128]{0:T(128)S(1)} %psum.66), channel_id=1, replica_groups=mesh['row'=16,'col'=32] {'col'}, use_global_device_ids=true, to_apply=%region_10.11 | all-reduce | flops 128 | bytes 1024 | tf_op jit(solution)/shard_map/psum | solution.py:73
  448.4 16.7 %collective-permute-start.11 = (f32[1,2,32,128]{2,3,1,0:T(8,128)S(1)}, f32[1,2,32,128]{2,3,1,0:T(8,128)S(1)}, u32[]{:S(2)}, u32[]{:S(2)}) collective-permute-start(f32[1,2,32,128]{2,3,1,0:T(8,128)S(1)} %bitcast.146), channel_id=1, source_target_pairs={{32,0},{64,32},{96,64},{128,96},{160,128},{192,160},{224,192},{256... | collective-permute-start | bytes 98312 | tf_op jit(solution)/shard_map/ppermute | solution.py:18
  465.2 1.9 collective-permute-start.10
  467.7 1.4 collective-permute-done.10
  469.2 1.3 collective-permute-start.12
  470.5 4.0 collective-permute-start.13
  476.2 99.8 %psum.68 = f32[128]{0:T(128)S(1)} all-reduce(f32[128]{0:T(128)S(1)} %fusion.10), channel_id=1, replica_groups=mesh['row'=16,'col'=32] {'row','col'}, use_global_device_ids=true, to_apply=%region_12.13 | all-reduce | flops 128 | bytes 1024 | tf_op jit(solution)/shard_map/psum | solution.py:84
  576.5 23.6 %psum.69 = f32[128]{0:T(128)S(1)} all-reduce(f32[128]{0:T(128)S(1)} %get-tuple-element.56), channel_id=1, replica_groups=mesh['row'=16,'col'=32] {'row'}, use_global_device_ids=true, to_apply=%region_14.15 | all-reduce | flops 128 | bytes 1024 | tf_op jit(solution)/shard_map/psum | solution.py:73
  600.1 59.7 %psum.70 = f32[128]{0:T(128)S(1)} all-reduce(f32[128]{0:T(128)S(1)} %psum.69), channel_id=1, replica_groups=mesh['row'=16,'col'=32] {'col'}, use_global_device_ids=true, to_apply=%region_15.16 | all-reduce | flops 128 | bytes 1024 | tf_op jit(solution)/shard_map/psum | solution.py:73
  659.9 16.7 %collective-permute-start.15 = (f32[1,2,32,128]{2,3,1,0:T(8,128)S(1)}, f32[1,2,32,128]{2,3,1,0:T(8,128)S(1)}, u32[]{:S(2)}, u32[]{:S(2)}) collective-permute-start(f32[1,2,32,128]{2,3,1,0:T(8,128)S(1)} %bitcast.153), channel_id=1, source_target_pairs={{32,0},{64,32},{96,64},{128,96},{160,128},{192,160},{224,192},{256... | collective-permute-start | bytes 98312 | tf_op jit(solution)/shard_map/ppermute | solution.py:18
  676.7 1.9 collective-permute-start.14
  679.2 1.4 collective-permute-done.14
  680.7 1.3 collective-permute-start.16
  682.0 4.0 collective-permute-start.17
  687.7 99.9 %psum.71 = f32[128]{0:T(128)S(1)} all-reduce(f32[128]{0:T(128)S(1)} %fusion.12), channel_id=1, replica_groups=mesh['row'=16,'col'=32] {'row','col'}, use_global_device_ids=true, to_apply=%region_17.18 | all-reduce | flops 128 | bytes 1024 | tf_op jit(solution)/shard_map/psum | solution.py:84
  (148 shorter events, 22.6 us)
Async XLA Ops:
  6.5 15.1 %copy-start.1 = (f32[1,2,128,128]{3,2,1,0:T(8,128)S(1)}, f32[1,2,128,128]{3,2,1,0:T(8,128)}, u32[]{:S(2)}) copy-start(f32[1,2,128,128]{3,2,1,0:T(8,128)} %param.15) | copy-start | bytes 393220
  6.5 11.8 %copy-start.4 = (f32[1,2,2,32]{3,2,1,0:T(2,128)S(1)}, f32[1,2,2,32]{3,2,1,0:T(2,128)}, u32[]{:S(2)}) copy-start(f32[1,2,2,32]{3,2,1,0:T(2,128)} %param.19) | copy-start | bytes 1540
  6.5 95.8 %all-gather.2.cloned.1.call-start = ((), (), s32[]{:S(2)}) async-start(), calls=%async_computation | async-start | bytes 1081344 | tf_op jit(solution)/shard_map/all_gather | solution.py:148
  7.6 21.3 %collective-permute-start.2 = (f32[1,2,32,128]{2,3,1,0:T(8,128)S(1)}, f32[1,2,32,128]{2,3,1,0:T(8,128)S(1)}, u32[]{:S(2)}, u32[]{:S(2)}) collective-permute-start(f32[1,2,32,128]{2,3,1,0:T(8,128)S(1)} %bitcast.150), channel_id=1, source_target_pairs={{32,0},{64,32},{96,64},{128,96},{160,128},{192,160},{224,192},{256... | collective-permute-start | bytes 98312 | tf_op jit(solution)/shard_map/ppermute | solution.py:18
  16.4 12.6 %collective-permute-start.1 = (f32[1,2,32,128]{2,3,1,0:T(8,128)S(1)}, f32[1,2,32,128]{2,3,1,0:T(8,128)S(1)}, u32[]{:S(2)}, u32[]{:S(2)}) collective-permute-start(f32[1,2,32,128]{2,3,1,0:T(8,128)S(1)} %bitcast.151), channel_id=1, source_target_pairs={{0,32},{32,64},{64,96},{96,128},{128,160},{160,192},{192,224},{224... | collective-permute-start | bytes 98312 | tf_op jit(solution)/shard_map/ppermute | solution.py:15
  18.4 10.5 %collective-permute-start = (f32[1,1,32]{2,1,0:T(1,128)S(1)}, f32[1,1,32]{2,1,0:T(1,128)S(1)}, u32[]{:S(2)}, u32[]{:S(2)}) collective-permute-start(f32[1,1,32]{2,1,0:T(1,128)S(1)} %slice_bitcast_fusion.1), channel_id=1, source_target_pairs={{0,1},{1,2},{2,3},{3,4},{4,5},{5,6},{6,7},{7,8},{8,9},{9,10},{10,1... | collective-permute-start | bytes 392 | tf_op jit(solution)/shard_map/ppermute | solution.py:26
  19.7 1.9 copy-start.10
  19.7 16.1 %collective-permute-start.5 = (f32[1,2,32]{2,1,0:T(2,128)S(1)}, f32[1,2,32]{2,1,0:T(2,128)S(1)}, u32[]{:S(2)}, u32[]{:S(2)}) collective-permute-start(f32[1,2,32]{2,1,0:T(2,128)S(1)} %bitcast.184), channel_id=1, source_target_pairs={{0,32},{32,64},{64,96},{96,128},{128,160},{160,192},{192,224},{224... | collective-permute-start | bytes 776 | tf_op jit(solution)/shard_map/ppermute | solution.py:26
  23.2 0.7 copy-start.5
  23.8 2.7 copy-start
  24.1 0.7 copy-start.9
  24.8 0.7 copy-start.6
  24.8 0.7 copy-start.7
  25.6 0.7 copy-start.8
  26.5 0.7 copy-start.3
  27.9 0.9 copy-start.2
  29.1 5.3 collective-permute-start.3
  30.4 5.2 collective-permute-start.4
  151.0 10.9 %collective-permute-start.7 = (f32[1,2,32,128]{2,3,1,0:T(8,128)S(1)}, f32[1,2,32,128]{2,3,1,0:T(8,128)S(1)}, u32[]{:S(2)}, u32[]{:S(2)}) collective-permute-start(f32[1,2,32,128]{2,3,1,0:T(8,128)S(1)} %bitcast.142), channel_id=1, source_target_pairs={{32,0},{64,32},{96,64},{128,96},{160,128},{192,160},{224,192},{256... | collective-permute-start | bytes 98312 | tf_op jit(solution)/shard_map/ppermute | solution.py:18
  157.9 5.1 collective-permute-start.6
  163.1 88.0 %collective-permute-start.8 = (f32[3,1,32,128]{3,2,1,0:T(8,128)S(1)}, f32[3,1,32,128]{3,2,1,0:T(8,128)S(1)}, u32[]{:S(2)}, u32[]{:S(2)}) collective-permute-start(f32[3,1,32,128]{3,2,1,0:T(8,128)S(1)} %get-tuple-element.43), channel_id=1, source_target_pairs={{1,0},{2,1},{3,2},{4,3},{5,4},{6,5},{7,6},{8,7},{9,8},{10,9},{11,1... | collective-permute-start | bytes 147464 | tf_op jit(solution)/shard_map/ppermute | solution.py:18
  164.4 86.7 %collective-permute-start.9 = (f32[3,1,32,128]{3,2,1,0:T(8,128)S(1)}, f32[3,1,32,128]{3,2,1,0:T(8,128)S(1)}, u32[]{:S(2)}, u32[]{:S(2)}) collective-permute-start(f32[3,1,32,128]{3,2,1,0:T(8,128)S(1)} %get-tuple-element.44), channel_id=1, source_target_pairs={{0,1},{1,2},{2,3},{3,4},{4,5},{5,6},{6,7},{7,8},{8,9},{9,10},{10,1... | collective-permute-start | bytes 147464 | tf_op jit(solution)/shard_map/ppermute | solution.py:15
  448.4 19.1 %collective-permute-start.11 = (f32[1,2,32,128]{2,3,1,0:T(8,128)S(1)}, f32[1,2,32,128]{2,3,1,0:T(8,128)S(1)}, u32[]{:S(2)}, u32[]{:S(2)}) collective-permute-start(f32[1,2,32,128]{2,3,1,0:T(8,128)S(1)} %bitcast.146), channel_id=1, source_target_pairs={{32,0},{64,32},{96,64},{128,96},{160,128},{192,160},{224,192},{256... | collective-permute-start | bytes 98312 | tf_op jit(solution)/shard_map/ppermute | solution.py:18
  465.2 3.9 collective-permute-start.10
  469.2 5.6 collective-permute-start.12
  470.5 5.3 collective-permute-start.13
  659.9 19.1 %collective-permute-start.15 = (f32[1,2,32,128]{2,3,1,0:T(8,128)S(1)}, f32[1,2,32,128]{2,3,1,0:T(8,128)S(1)}, u32[]{:S(2)}, u32[]{:S(2)}) collective-permute-start(f32[1,2,32,128]{2,3,1,0:T(8,128)S(1)} %bitcast.153), channel_id=1, source_target_pairs={{32,0},{64,32},{96,64},{128,96},{160,128},{192,160},{224,192},{256... | collective-permute-start | bytes 98312 | tf_op jit(solution)/shard_map/ppermute | solution.py:18
  676.7 3.9 collective-permute-start.14
  680.7 5.6 collective-permute-start.16
  682.0 5.3 collective-permute-start.17
Sparse Core Ops, SparseCore 0:
  23.1 79.1 all-gather.1
